TPU v7x, 32 devices: a whole 2x2x4 slice. The times are simulated.
32 devices in a mesh: groups: 2 (over x), tile: 16 (over z, y, core).
Axes of the slice: x: 2, y: 2, z: 4, core: 2. Of those that a mesh axis runs over, the one named last changes fastest.
Arguments:
- fine_nodes: bfloat16 [32768, 512], P(('groups', 'tile')), parts along dimension 0, may hold values from -6 to 6
- fine_table: int32 [16384, 6], P('tile'), may hold values from 0 to 16383, as said below
- mid_table: int32 [4096, 6], P('tile'), may hold values from 0 to 4095, as said below
- coarse_table: int32 [1024, 6], replicated, may hold values from 0 to 1023, as said below
- fine_parent: int32 [16384], P('tile'), may hold values from 0 to 4095, as said below
- mid_parent: int32 [4096], P('tile'), may hold values from 0 to 1023, as said below
- edge_self: bfloat16 [3, 512, 512], replicated, may hold values from -0.1875 to 0.1875
- edge_peer: bfloat16 [3, 512, 512], replicated, may hold values from -0.1875 to 0.1875
- edge_bias: float32 [3, 512], replicated, may hold values from -3 to 3
- node_self: bfloat16 [3, 512, 512], replicated, may hold values from -0.1875 to 0.1875
- node_message: bfloat16 [3, 512, 512], replicated, may hold values from -0.109375 to 0.109375
- node_bias: float32 [3, 512], replicated, may hold values from -3 to 3
- node_out: bfloat16 [3, 512, 512], replicated, may hold values from -0.25 to 0.25
- ascend_gain: float32 [2, 512], replicated, may hold values from 0.1 to 1.9
- down_self: bfloat16 [2, 512, 512], replicated, may hold values from -0.1875 to 0.1875
- down_parent: bfloat16 [2, 512, 512], replicated, may hold values from -0.1875 to 0.1875
- down_bias: float32 [2, 512], replicated, may hold values from -3 to 3
- down_out: bfloat16 [2, 512, 512], replicated, may hold values from -0.25 to 0.25
Outputs:
- fine_out: bfloat16 [32768, 512], P(('groups', 'tile')), parts along dimension 0
- mid_out: bfloat16 [8192, 512], P(('groups', 'tile')), parts along dimension 0
- coarse_out: bfloat16 [2048, 512], P(('groups', 'tile')), parts along dimension 0
There are 2 independent parts, one for each index of `groups`. A program takes and returns all parts, laid end to end along the dimension named above; an argument that names none is the same for every part. Nothing has to cross between parts.
Inputs may be any that keep to these rules, and one draw needn't show every extreme that they name: `fine_table`: fine node n is grid cell (n // 256, n % 256); each of its six neighbours lies in its own grid row or one of the two rows beside it, columns wrapping around. `mid_table`: Level-1 node p is cell (p // 128, p % 128); each neighbour lies in its own row or one of the two rows beside it, columns wrapping around. `coarse_table`: any level-2 nodes. `fine_parent`: the parent of fine cell (r, c) lies in level-1 row r // 2 - 1, r // 2 or r // 2 + 1. `mid_parent`: the parent of level-1 cell (r, c) lies in level-2 row r // 2 - 1, r // 2 or r // 2 + 1.
All inputs are finite; a program needn't handle non-finite values.
Results may differ from a plain program's by a relative error of at most 0.014.
Values may be sent and summed in bfloat16 or wider, within the bound.
A program may use at most 64 MiB of HBM per device.

v0:
```python
import jax
import jax.numpy as jnp
from jax import lax
from jax.sharding import PartitionSpec as P

COLS = 256


def with_halo(cells, sides, width):
    for axis, dim in sides:
        count = lax.axis_size(axis)
        ends = count - 1
        head = lax.slice_in_dim(cells, 0, width, axis=dim)
        tail = lax.slice_in_dim(cells, cells.shape[dim] - width, cells.shape[dim], axis=dim)
        cells = jnp.concatenate(
            [
                lax.ppermute(tail, axis, [(i, (i + 1) % count) for i in range(ends)]),
                cells,
                lax.ppermute(head, axis, [((i + 1) % count, i) for i in range(ends)]),
            ],
            axis=dim,
        )
    return cells


def gelu_tanh(values):
    return jax.nn.gelu(values, approximate=True)


def rim_rows(block_rows, col_count):
    feature_count = block_rows.shape[1]
    grid_rows = block_rows.reshape(block_rows.shape[0] // col_count, col_count, feature_count)
    padded = with_halo(grid_rows, (("tile", 0),), 1)
    return padded.reshape(-1, feature_count)


def finish_level(node_rows, summed, level_index, weights):
    node_self = weights[3]
    node_message = weights[4]
    node_bias = weights[5]
    node_out = weights[6]
    message = summed.astype(jnp.bfloat16)
    pre_act = jnp.dot(node_rows, node_self[level_index], preferred_element_type=jnp.float32)
    pre_act = (
        pre_act
        + jnp.dot(message, node_message[level_index], preferred_element_type=jnp.float32)
        + node_bias[level_index]
    )
    hidden = gelu_tanh(pre_act).astype(jnp.bfloat16)
    result = node_rows.astype(jnp.float32) + jnp.dot(
        hidden, node_out[level_index], preferred_element_type=jnp.float32
    )
    return result.astype(jnp.bfloat16)


def own_projection(node_rows, level_index, weights):
    return (
        jnp.dot(node_rows, weights[0][level_index], preferred_element_type=jnp.float32)
        + weights[2][level_index]
    )


def peer_projection(node_rows, level_index, weights):
    return jnp.dot(node_rows, weights[1][level_index], preferred_element_type=jnp.float32).astype(
        jnp.bfloat16
    )


def process_local(node_rows, neighbours, level_index, col_count, weights):
    own_proj = own_projection(node_rows, level_index, weights)
    extended = rim_rows(peer_projection(node_rows, level_index, weights), col_count)
    offset = lax.axis_index("tile") * node_rows.shape[0] - col_count
    local_ids = neighbours - offset
    summed = jnp.zeros(own_proj.shape, jnp.float32)
    for slot_index in range(6):
        fetched = extended[local_ids[:, slot_index]].astype(jnp.float32)
        summed = summed + gelu_tanh(own_proj + fetched)
    return finish_level(node_rows, summed, level_index, weights)


def ascend_local(children, parents, col_up, gain_vec):
    feature_count = children.shape[1]
    rows_up = children.shape[0] // (4 * col_up)
    span_rows = (rows_up + 2) * col_up
    offset = lax.axis_index("tile") * rows_up * col_up - col_up
    local_ids = parents - offset
    onehot = (local_ids[None, :] == jnp.arange(span_rows, dtype=jnp.int32)[:, None]).astype(
        jnp.bfloat16
    )
    partial_value = jnp.dot(onehot, children, preferred_element_type=jnp.float32)
    grid_rows = partial_value.reshape(rows_up + 2, col_up, feature_count)
    padded = with_halo(grid_rows.astype(jnp.bfloat16), (("tile", 0),), 1).astype(grid_rows.dtype)
    summed = grid_rows[1:-1]
    summed = summed.at[0].add(padded[0])
    summed = summed.at[-1].add(padded[-1])
    summed = summed.reshape(rows_up * col_up, feature_count)
    scale_inv = lax.rsqrt(jnp.mean(summed * summed, axis=1, keepdims=True) + 1e-05)
    return (summed * scale_inv * gain_vec).astype(jnp.bfloat16)


def descend_local(children, lifted_ext, parents, col_up, level_index, downs):
    down_self, down_parent, down_bias, down_out = downs
    rows_up = children.shape[0] // (4 * col_up)
    offset = lax.axis_index("tile") * rows_up * col_up - col_up
    fetched = lifted_ext[parents - offset].astype(jnp.float32)
    pre_act = (
        jnp.dot(children, down_self[level_index], preferred_element_type=jnp.float32)
        + fetched
        + down_bias[level_index]
    )
    hidden = gelu_tanh(pre_act).astype(jnp.bfloat16)
    result = children.astype(jnp.float32) + jnp.dot(
        hidden, down_out[level_index], preferred_element_type=jnp.float32
    )
    return result.astype(jnp.bfloat16)


def local(
    fine_nodes,
    fine_table,
    mid_table,
    coarse_table,
    fine_parent,
    mid_parent,
    edge_self,
    edge_peer,
    edge_bias,
    node_self,
    node_message,
    node_bias,
    node_out,
    ascend_gain,
    down_self,
    down_parent,
    down_bias,
    down_out,
):
    weights = (edge_self, edge_peer, edge_bias, node_self, node_message, node_bias, node_out)
    downs = (down_self, down_parent, down_bias, down_out)
    col_mid = COLS // 2
    col_low = COLS // 4
    fine_rows = process_local(fine_nodes, fine_table, 0, COLS, weights)
    mid_start = ascend_local(fine_rows, fine_parent, col_mid, ascend_gain[0])
    mid_rows = process_local(mid_start, mid_table, 1, col_mid, weights)
    coarse_start = ascend_local(mid_rows, mid_parent, col_low, ascend_gain[1])
    coarse_count = coarse_start.shape[0]
    peer_proj = peer_projection(coarse_start, 2, weights)
    own_proj = own_projection(coarse_start, 2, weights)
    my_table = lax.dynamic_slice_in_dim(
        coarse_table, lax.axis_index("tile") * coarse_count, coarse_count, 0
    )
    running = jnp.zeros(own_proj.shape, jnp.float32)
    fragment = lax.all_gather(peer_proj, "tile", axis=0, tiled=True)
    row_count = fragment.shape[0]
    for slot_index in range(6):
        where_ids = my_table[:, slot_index]
        inside = (where_ids >= 0) & (where_ids < row_count)
        fetched = fragment[jnp.clip(where_ids, 0, row_count - 1)].astype(jnp.float32)
        running = running + jnp.where(inside[:, None], gelu_tanh(own_proj + fetched), 0.0)
    coarse_final = finish_level(coarse_start, running, 2, weights)
    lifted_own = jnp.dot(coarse_final, down_parent[1], preferred_element_type=jnp.float32).astype(
        jnp.bfloat16
    )
    lifted_ext = rim_rows(lifted_own, col_low)
    mid_final = descend_local(mid_rows, lifted_ext, mid_parent, col_low, 1, downs)
    lifted_mid = rim_rows(
        jnp.dot(mid_final, down_parent[0], preferred_element_type=jnp.float32).astype(jnp.bfloat16),
        col_mid,
    )
    fine_final = descend_local(fine_rows, lifted_mid, fine_parent, col_mid, 0, downs)
    return (fine_final, mid_final, coarse_final)


def solution(mesh):
    placed = (
        P(("groups", "tile"), None),
        P("tile", None),
        P("tile", None),
        P(),
        P("tile"),
        P("tile"),
        P(),
        P(),
        P(),
        P(),
        P(),
        P(),
        P(),
        P(),
        P(),
        P(),
        P(),
        P(),
    )
    return jax.shard_map(
        local,
        mesh=mesh,
        in_specs=placed,
        out_specs=(
            P(("groups", "tile"), None),
            P(("groups", "tile"), None),
            P(("groups", "tile"), None),
        ),
        check_vma=False,
    )
```

profile of v0, /device:TPU:5, one launch (start us, length us, event | category | flops | bytes accessed | tf_op | source)
XLA Modules:
  0.0 196.6 jit_solution(9857290049073583987)
XLA Ops:
  7.3 2.1 %convolution_convert_fusion = bf16[1024,512]{1,0:T(8,128)(2,1)S(1)} fusion(bf16[1024,512]{1,0:T(8,128)(2,1)} %param.26, bf16[3,512,512]{2,1,0:T(8,128)(2,1)} %param.33), kind=kOutput, calls=%fused_computation.97 | convolution fusion | flops 537395200 | bytes 2621440 | tf_op jit(solution)/shard_map/dot_general | solution.py:64
  9.5 3.8 %collective-permute-start = (bf16[1,256,512]{2,1,0:T(8,128)(2,1)S(1)}, bf16[1,256,512]{2,1,0:T(8,128)(2,1)S(1)}, u32[]{:S(2)}, u32[]{:S(2)}) collective-permute-start(bf16[1,256,512]{2,1,0:T(8,128)(2,1)S(1)} %get-tuple-element.57), channel_id=1, source_target_pairs={{0,1},{1,2},{2,3},{3,4},{4,5},{5,6},{6,7},{7,8},{8,9},{9,10},{10,1... | collective-permute-start | bytes 786440 | tf_op jit(solution)/shard_map/ppermute | solution.py:17
  13.4 1.9 collective-permute-start.1
  15.5 3.1 %fusion.175 = f32[1024,512]{1,0:T(8,128)} fusion(bf16[1024,512]{1,0:T(8,128)(2,1)S(1)} %copy-done.3, bf16[3,512,512]{2,1,0:T(8,128)(2,1)} %param.35), kind=kOutput, calls=%fused_computation.221 | convolution fusion | flops 536870912 | bytes 3670016 | tf_op jit(solution)/shard_map/dot_general | solution.py:43
  18.7 3.2 %collective-permute-done.1 = bf16[1,256,512]{2,1,0:T(8,128)(2,1)S(1)} collective-permute-done((bf16[1,256,512]{2,1,0:T(8,128)(2,1)S(1)}, bf16[1,256,512]{2,1,0:T(8,128)(2,1)S(1)}, u32[]{:S(2)}, u32[]{:S(2)}) %collective-permute-start.1) | collective-permute-done | bytes 262176 | tf_op jit(solution)/shard_map/ppermute | solution.py:19
  21.9 0.2 pad_maximum_fusion
  22.1 5.1 %gather_fusion = bf16[1024,512]{1,0:T(8,128)(2,1)} fusion(bf16[1536,512]{1,0:T(8,128)(2,1)S(1)} %bitcast.201, s32[1024]{0:T(1024)S(1)} %broadcast_clamp_fusion.5), kind=kCustom, calls=%fused_computation | custom fusion | bytes 2101248 | tf_op jit(solution)/shard_map/gather | solution.py:76
  27.2 5.1 %gather_fusion.1 = bf16[1024,512]{1,0:T(8,128)(2,1)} fusion(bf16[1536,512]{1,0:T(8,128)(2,1)S(1)} %bitcast.202, s32[1024]{0:T(1024)S(1)} %broadcast_clamp_fusion.4), kind=kCustom, calls=%fused_computation.1 | custom fusion | bytes 2101248 | tf_op jit(solution)/shard_map/gather | solution.py:76
  32.3 5.1 %gather_fusion.2 = bf16[1024,512]{1,0:T(8,128)(2,1)} fusion(bf16[1536,512]{1,0:T(8,128)(2,1)S(1)} %bitcast.203, s32[1024]{0:T(1024)S(1)} %broadcast_clamp_fusion.3), kind=kCustom, calls=%fused_computation.2 | custom fusion | bytes 2101248 | tf_op jit(solution)/shard_map/gather | solution.py:76
  37.4 5.0 %gather_fusion.3 = bf16[1024,512]{1,0:T(8,128)(2,1)} fusion(bf16[1536,512]{1,0:T(8,128)(2,1)S(1)} %bitcast.204, s32[1024]{0:T(1024)S(1)} %broadcast_clamp_fusion.2), kind=kCustom, calls=%fused_computation.3 | custom fusion | bytes 2101248 | tf_op jit(solution)/shard_map/gather | solution.py:76
  42.4 5.1 %gather_fusion.4 = bf16[1024,512]{1,0:T(8,128)(2,1)} fusion(bf16[1536,512]{1,0:T(8,128)(2,1)S(1)} %bitcast.205, s32[1024]{0:T(1024)S(1)} %broadcast_clamp_fusion.1), kind=kCustom, calls=%fused_computation.4 | custom fusion | bytes 2101248 | tf_op jit(solution)/shard_map/gather | solution.py:76
  47.5 5.1 %gather_fusion.5 = bf16[1024,512]{1,0:T(8,128)(2,1)} fusion(bf16[1536,512]{1,0:T(8,128)(2,1)S(1)} %bitcast.206, s32[1024]{0:T(1024)S(1)} %broadcast_clamp_fusion), kind=kCustom, calls=%fused_computation.5 | custom fusion | bytes 2101248 | tf_op jit(solution)/shard_map/gather | solution.py:76
  52.5 10.0 %fusion.54 = bf16[1024,512]{1,0:T(8,128)(2,1)S(1)} fusion(f32[1024,512]{1,0:T(8,128)} %fusion.175, f32[512]{0:T(512)S(1)} %bitcast.245, bf16[1024,512]{1,0:T(8,128)(2,1)} %gather_fusion.5, bf16[1024,512]{1,0:T(8,128)(2,1)} %gather_fusion.4, bf16[1024,512]{1,0:T(8,128)(2,1)} %gather_fusion.3, bf16[1024,512]{1,0:T(8,128)(2,1)} %gather_fusion.2, ...), kind=kOutput, calls=%fused_computation.82 | convolution fusion | flops 1114636288 | bytes 11538432 | tf_op jit(solution)/shard_map/dot_general | solution.py:46
  62.5 1.7 add_convert_fusion.1
  64.3 0.7 fusion.343
  65.1 1.9 collective-permute-start.2
  67.0 2.6 %collective-permute-start.3 = (bf16[1,128,512]{2,1,0:T(8,128)(2,1)S(1)}, bf16[1,128,512]{2,1,0:T(8,128)(2,1)S(1)}, u32[]{:S(2)}, u32[]{:S(2)}) collective-permute-start(bf16[1,128,512]{2,1,0:T(8,128)(2,1)S(1)} %get-tuple-element.60), channel_id=1, source_target_pairs={{1,0},{2,1},{3,2},{4,3},{5,4},{6,5},{7,6},{8,7},{9,8},{10,9},{11,1... | collective-permute-start | bytes 393224 | tf_op jit(solution)/shard_map/ppermute | solution.py:19
  69.7 4.5 %collective-permute-done.3 = bf16[1,128,512]{2,1,0:T(8,128)(2,1)S(1)} collective-permute-done((bf16[1,128,512]{2,1,0:T(8,128)(2,1)S(1)}, bf16[1,128,512]{2,1,0:T(8,128)(2,1)S(1)}, u32[]{:S(2)}, u32[]{:S(2)}) %collective-permute-start.3) | collective-permute-done | bytes 131104 | tf_op jit(solution)/shard_map/ppermute | solution.py:19
  74.3 0.1 multiply_reduce_fusion
  74.4 0.1 multiply_convert_fusion
  74.5 1.5 convolution_convert_fusion.2
  76.0 0.3 fusion.160
  76.4 1.9 collective-permute-start.4
  78.3 2.4 %collective-permute-start.5 = (bf16[1,128,512]{2,1,0:T(8,128)(2,1)S(1)}, bf16[1,128,512]{2,1,0:T(8,128)(2,1)S(1)}, u32[]{:S(2)}, u32[]{:S(2)}) collective-permute-start(bf16[1,128,512]{2,1,0:T(8,128)(2,1)S(1)} %get-tuple-element.64), channel_id=1, source_target_pairs={{1,0},{2,1},{3,2},{4,3},{5,4},{6,5},{7,6},{8,7},{9,8},{10,9},{11,1... | collective-permute-start | bytes 393224 | tf_op jit(solution)/shard_map/ppermute | solution.py:19
  80.7 1.3 convolution_add_fusion.3
  82.1 0.8 fusion.163
  82.9 2.6 %collective-permute-done.5 = bf16[1,128,512]{2,1,0:T(8,128)(2,1)S(1)} collective-permute-done((bf16[1,128,512]{2,1,0:T(8,128)(2,1)S(1)}, bf16[1,128,512]{2,1,0:T(8,128)(2,1)S(1)}, u32[]{:S(2)}, u32[]{:S(2)}) %collective-permute-start.5) | collective-permute-done | bytes 131104 | tf_op jit(solution)/shard_map/ppermute | solution.py:19
  85.5 1.2 gather_fusion.10
  86.7 1.9 gather_fusion.6
  88.6 1.9 gather_fusion.7
  90.4 1.9 gather_fusion.8
  92.3 1.9 gather_fusion.9
  94.2 1.9 gather_fusion.11
  96.0 3.3 %fusion.66 = bf16[256,512]{1,0:T(8,128)(2,1)S(1)} fusion(f32[256,512]{1,0:T(8,128)S(1)} %fusion.160, bf16[3,512,512]{2,1,0:T(8,128)(2,1)} %param.38, bf16[3,512,512]{2,1,0:T(8,128)(2,1)} %param.36, bf16[256,512]{1,0:T(8,128)(2,1)} %fusion.163, f32[256,512]{1,0:T(8,128)S(1)} %convolution_add_fusion.3, bf16[256,512]{1,0:T(8,128)(2,1)} %gather_fusion.11, ...), kind=kOutput, calls=%fused_computation.103 | convolution fusion | flops 278921216 | bytes 4196352 | tf_op jit(solution)/shard_map/dot_general | solution.py:50
  99.3 0.2 fusion.344
  99.5 1.9 collective-permute-start.6
  101.5 2.4 %collective-permute-start.7 = (bf16[1,64,512]{2,1,0:T(8,128)(2,1)S(1)}, bf16[1,64,512]{2,1,0:T(8,128)(2,1)S(1)}, u32[]{:S(2)}, u32[]{:S(2)}) collective-permute-start(bf16[1,64,512]{2,1,0:T(8,128)(2,1)S(1)} %get-tuple-element.66), channel_id=1, source_target_pairs={{1,0},{2,1},{3,2},{4,3},{5,4},{6,5},{7,6},{8,7},{9,8},{10,9},{11,1... | collective-permute-start | bytes 196616 | tf_op jit(solution)/shard_map/ppermute | solution.py:19
  103.9 4.1 %collective-permute-done.7 = bf16[1,64,512]{2,1,0:T(8,128)(2,1)S(1)} collective-permute-done((bf16[1,64,512]{2,1,0:T(8,128)(2,1)S(1)}, bf16[1,64,512]{2,1,0:T(8,128)(2,1)S(1)}, u32[]{:S(2)}, u32[]{:S(2)}) %collective-permute-start.7) | collective-permute-done | bytes 65568 | tf_op jit(solution)/shard_map/ppermute | solution.py:19
  107.9 0.1 multiply_reduce_fusion.1
  108.1 0.1 multiply_convert_fusion.1
  108.2 1.9 convolution_convert_fusion.4
  110.1 0.1 constant_dynamic-slice_fusion
  110.3 0.2 fusion.151
  110.5 36.7 %all-gather.2.cloned.1.call-done = bf16[1024,512]{1,0:T(8,128)(2,1)} async-done(((bf16[64,512]{1,0:T(8,128)(2,1)}), bf16[1024,512]{1,0:T(8,128)(2,1)}) %all-gather.2.cloned.1.call-update) | async-done | bytes 1048592 | tf_op jit(solution)/shard_map/all_gather | solution.py:153
  147.2 2.2 %gather_fusion.12 = bf16[64,512]{1,0:T(8,128)(2,1)S(1)} fusion(bf16[1024,512]{1,0:T(8,128)(2,1)} %all-gather.2.cloned.1.call-done, s32[1024]{0:T(1024)S(1)} %get-tuple-element.112), kind=kCustom, calls=%fused_computation.12 | custom fusion | bytes 131328 | tf_op jit(solution)/shard_map/gather | solution.py:158
  149.3 2.1 %gather_fusion.13 = bf16[64,512]{1,0:T(8,128)(2,1)S(1)} fusion(bf16[1024,512]{1,0:T(8,128)(2,1)} %all-gather.2.cloned.1.call-done, s32[1024]{0:T(1024)S(1)} %get-tuple-element.111), kind=kCustom, calls=%fused_computation.13 | custom fusion | bytes 131328 | tf_op jit(solution)/shard_map/gather | solution.py:158
  151.4 2.1 %gather_fusion.14 = bf16[64,512]{1,0:T(8,128)(2,1)S(1)} fusion(bf16[1024,512]{1,0:T(8,128)(2,1)} %all-gather.2.cloned.1.call-done, s32[1024]{0:T(1024)S(1)} %get-tuple-element.110), kind=kCustom, calls=%fused_computation.14 | custom fusion | bytes 131328 | tf_op jit(solution)/shard_map/gather | solution.py:158
  153.5 0.7 gather_fusion.15
  154.2 0.7 gather_fusion.16
  154.9 0.7 gather_fusion.17
  155.6 1.7 fusion.297
  157.3 1.6 fusion.69
  158.9 0.2 fusion.70
  159.1 3.4 %collective-permute-start.8 = (bf16[1,64,512]{2,1,0:T(8,128)(2,1)S(1)}, bf16[1,64,512]{2,1,0:T(8,128)(2,1)S(1)}, u32[]{:S(2)}, u32[]{:S(2)}) collective-permute-start(bf16[1,64,512]{2,1,0:T(8,128)(2,1)S(1)} %fusion.70), channel_id=1, source_target_pairs={{0,1},{1,2},{2,3},{3,4},{4,5},{5,6},{6,7},{7,8},{8,9},{9,10},{10,1... | collective-permute-start | bytes 196616 | tf_op jit(solution)/shard_map/ppermute | solution.py:17
  162.6 1.9 collective-permute-start.9
  164.5 4.5 %collective-permute-done.9 = bf16[1,64,512]{2,1,0:T(8,128)(2,1)S(1)} collective-permute-done((bf16[1,64,512]{2,1,0:T(8,128)(2,1)S(1)}, bf16[1,64,512]{2,1,0:T(8,128)(2,1)S(1)}, u32[]{:S(2)}, u32[]{:S(2)}) %collective-permute-start.9) | collective-permute-done | bytes 65568 | tf_op jit(solution)/shard_map/ppermute | solution.py:19
  169.1 1.2 gather_fusion.18
  170.2 1.7 fusion.67
  171.9 0.3 convolution_convert_fusion.1
  172.3 1.9 collective-permute-start.10
  174.2 2.4 %collective-permute-start.11 = (bf16[1,128,512]{2,1,0:T(8,128)(2,1)S(1)}, bf16[1,128,512]{2,1,0:T(8,128)(2,1)S(1)}, u32[]{:S(2)}, u32[]{:S(2)}) collective-permute-start(bf16[1,128,512]{2,1,0:T(8,128)(2,1)S(1)} %get-tuple-element.62), channel_id=1, source_target_pairs={{1,0},{2,1},{3,2},{4,3},{5,4},{6,5},{7,6},{8,7},{9,8},{10,9},{11,1... | collective-permute-start | bytes 393224 | tf_op jit(solution)/shard_map/ppermute | solution.py:19
  176.6 4.8 %collective-permute-done.11 = bf16[1,128,512]{2,1,0:T(8,128)(2,1)S(1)} collective-permute-done((bf16[1,128,512]{2,1,0:T(8,128)(2,1)S(1)}, bf16[1,128,512]{2,1,0:T(8,128)(2,1)S(1)}, u32[]{:S(2)}, u32[]{:S(2)}) %collective-permute-start.11) | collective-permute-done | bytes 131104 | tf_op jit(solution)/shard_map/ppermute | solution.py:19
  181.4 4.0 %gather_fusion.19 = bf16[1024,512]{1,0:T(8,128)(2,1)S(1)} fusion(bf16[512,512]{1,0:T(8,128)(2,1)S(1)} %bitcast.213, s32[1024]{0:T(1024)S(1)} %get-tuple-element.51), kind=kCustom, calls=%fused_computation.19 | custom fusion | bytes 2101248 | tf_op jit(solution)/shard_map/gather | solution.py:105
  185.4 4.3 %add_convert_fusion = bf16[1024,512]{1,0:T(8,128)(2,1)} fusion(bf16[1024,512]{1,0:T(8,128)(2,1)} %copy-done.17, bf16[1024,512]{1,0:T(8,128)(2,1)S(1)} %gather_fusion.19, f32[512]{0:T(512)S(1)} %bitcast.244, bf16[2,512,512]{2,1,0:T(8,128)(2,1)S(1)} %copy-done.15, bf16[2,512,512]{2,1,0:T(8,128)(2,1)} %param.40), kind=kOutput, calls=%fused_computation.91 | convolution fusion | flops 1081606144 | bytes 5244928 | tf_op jit(solution)/shard_map/dot_general | solution.py:112
  (85 shorter events, 0.8 us)
Async XLA Ops:
  7.2 102.9 %copy-start = (s32[1024,6]{0,1:T(8,128)S(1)}, s32[1024,6]{0,1:T(8,128)}, u32[]{:S(2)}) copy-start(s32[1024,6]{0,1:T(8,128)} %param.29) | copy-start | bytes 73732
  7.2 8.3 %copy-start.3 = (bf16[1024,512]{1,0:T(8,128)(2,1)S(1)}, bf16[1024,512]{1,0:T(8,128)(2,1)}, u32[]{:S(2)}) copy-start(bf16[1024,512]{1,0:T(8,128)(2,1)} %param.26) | copy-start | bytes 3145732
  7.2 8.1 %copy-start.7 = (s32[1024,6]{0,1:T(8,128)S(1)}, s32[1024,6]{0,1:T(8,128)}, u32[]{:S(2)}) copy-start(s32[1024,6]{0,1:T(8,128)} %param.27) | copy-start | bytes 73732
  7.2 8.2 %copy-start.9 = (f32[3,512]{1,0:T(4,128)S(1)}, f32[3,512]{1,0:T(4,128)}, u32[]{:S(2)}) copy-start(f32[3,512]{1,0:T(4,128)} %param.37) | copy-start | bytes 18436
  7.2 139.9 %all-gather.2.cloned.1.call-start = ((), (), s32[]{:S(2)}) async-start(), calls=%async_computation | async-start | bytes 1114112 | tf_op jit(solution)/shard_map/all_gather | solution.py:153
  9.4 9.1 %copy-start.12 = (f32[2,512]{1,0:T(2,128)S(1)}, f32[2,512]{1,0:T(2,128)}, u32[]{:S(2)}) copy-start(f32[2,512]{1,0:T(2,128)} %param.39) | copy-start | bytes 12292
  9.5 9.1 %copy-start.11 = (s32[1024]{0:T(1024)S(1)}, s32[1024]{0:T(1024)}, u32[]{:S(2)}) copy-start(s32[1024]{0:T(1024)} %param.30) | copy-start | bytes 12292
  9.5 9.1 %copy-start.8 = (s32[256,6]{0,1:T(8,128)S(1)}, s32[256,6]{0,1:T(8,128)}, u32[]{:S(2)}) copy-start(s32[256,6]{0,1:T(8,128)} %param.28) | copy-start | bytes 18436
  9.5 9.2 %copy-start.14 = (s32[256]{0:T(256)S(1)}, s32[256]{0:T(256)}, u32[]{:S(2)}) copy-start(s32[256]{0:T(256)} %param.31) | copy-start | bytes 3076
  9.5 9.2 %copy-start.10 = (f32[3,512]{1,0:T(4,128)S(1)}, f32[3,512]{1,0:T(4,128)}, u32[]{:S(2)}) copy-start(f32[3,512]{1,0:T(4,128)} %param.34) | copy-start | bytes 18436
  9.5 9.2 %collective-permute-start = (bf16[1,256,512]{2,1,0:T(8,128)(2,1)S(1)}, bf16[1,256,512]{2,1,0:T(8,128)(2,1)S(1)}, u32[]{:S(2)}, u32[]{:S(2)}) collective-permute-start(bf16[1,256,512]{2,1,0:T(8,128)(2,1)S(1)} %get-tuple-element.57), channel_id=1, source_target_pairs={{0,1},{1,2},{2,3},{3,4},{4,5},{5,6},{6,7},{7,8},{8,9},{9,10},{10,1... | collective-permute-start | bytes 786440 | tf_op jit(solution)/shard_map/ppermute | solution.py:17
  13.4 8.6 %collective-permute-start.1 = (bf16[1,256,512]{2,1,0:T(8,128)(2,1)S(1)}, bf16[1,256,512]{2,1,0:T(8,128)(2,1)S(1)}, u32[]{:S(2)}, u32[]{:S(2)}) collective-permute-start(bf16[1,256,512]{2,1,0:T(8,128)(2,1)S(1)} %get-tuple-element.58), channel_id=1, source_target_pairs={{1,0},{2,1},{3,2},{4,3},{5,4},{6,5},{7,6},{8,7},{9,8},{10,9},{11,1... | collective-permute-start | bytes 786440 | tf_op jit(solution)/shard_map/ppermute | solution.py:19
  47.5 5.1 %copy-start.4 = (bf16[1024,512]{1,0:T(8,128)(2,1)S(1)}, bf16[1024,512]{1,0:T(8,128)(2,1)}, u32[]{:S(2)}) copy-start(bf16[1024,512]{1,0:T(8,128)(2,1)} %param.26) | copy-start | bytes 3145732
  64.3 5.4 %copy-start.17 = (bf16[1024,512]{1,0:T(8,128)(2,1)}, bf16[1024,512]{1,0:T(8,128)(2,1)S(1)}, u32[]{:S(2)}) copy-start(bf16[1024,512]{1,0:T(8,128)(2,1)S(1)} %add_convert_fusion.1) | copy-start | bytes 3145732
  65.1 4.6 %collective-permute-start.2 = (bf16[1,128,512]{2,1,0:T(8,128)(2,1)S(1)}, bf16[1,128,512]{2,1,0:T(8,128)(2,1)S(1)}, u32[]{:S(2)}, u32[]{:S(2)}) collective-permute-start(bf16[1,128,512]{2,1,0:T(8,128)(2,1)S(1)} %get-tuple-element.59), channel_id=1, source_target_pairs={{0,1},{1,2},{2,3},{3,4},{4,5},{5,6},{6,7},{7,8},{8,9},{9,10},{10,1... | collective-permute-start | bytes 393224 | tf_op jit(solution)/shard_map/ppermute | solution.py:17
  67.0 7.2 %collective-permute-start.3 = (bf16[1,128,512]{2,1,0:T(8,128)(2,1)S(1)}, bf16[1,128,512]{2,1,0:T(8,128)(2,1)S(1)}, u32[]{:S(2)}, u32[]{:S(2)}) collective-permute-start(bf16[1,128,512]{2,1,0:T(8,128)(2,1)S(1)} %get-tuple-element.60), channel_id=1, source_target_pairs={{1,0},{2,1},{3,2},{4,3},{5,4},{6,5},{7,6},{8,7},{9,8},{10,9},{11,1... | collective-permute-start | bytes 393224 | tf_op jit(solution)/shard_map/ppermute | solution.py:19
  74.2 1.8 copy-start.2
  76.4 6.5 %collective-permute-start.4 = (bf16[1,128,512]{2,1,0:T(8,128)(2,1)S(1)}, bf16[1,128,512]{2,1,0:T(8,128)(2,1)S(1)}, u32[]{:S(2)}, u32[]{:S(2)}) collective-permute-start(bf16[1,128,512]{2,1,0:T(8,128)(2,1)S(1)} %get-tuple-element.63), channel_id=1, source_target_pairs={{0,1},{1,2},{2,3},{3,4},{4,5},{5,6},{6,7},{7,8},{8,9},{9,10},{10,1... | collective-permute-start | bytes 393224 | tf_op jit(solution)/shard_map/ppermute | solution.py:17
  78.3 7.2 %collective-permute-start.5 = (bf16[1,128,512]{2,1,0:T(8,128)(2,1)S(1)}, bf16[1,128,512]{2,1,0:T(8,128)(2,1)S(1)}, u32[]{:S(2)}, u32[]{:S(2)}) collective-permute-start(bf16[1,128,512]{2,1,0:T(8,128)(2,1)S(1)} %get-tuple-element.64), channel_id=1, source_target_pairs={{1,0},{2,1},{3,2},{4,3},{5,4},{6,5},{7,6},{8,7},{9,8},{10,9},{11,1... | collective-permute-start | bytes 393224 | tf_op jit(solution)/shard_map/ppermute | solution.py:19
  99.3 11.0 %copy-start.13 = (f32[2,512]{1,0:T(2,128)S(1)}, f32[2,512]{1,0:T(2,128)}, u32[]{:S(2)}) copy-start(f32[2,512]{1,0:T(2,128)} %param.42) | copy-start | bytes 12292
  99.5 4.3 %collective-permute-start.6 = (bf16[1,64,512]{2,1,0:T(8,128)(2,1)S(1)}, bf16[1,64,512]{2,1,0:T(8,128)(2,1)S(1)}, u32[]{:S(2)}, u32[]{:S(2)}) collective-permute-start(bf16[1,64,512]{2,1,0:T(8,128)(2,1)S(1)} %get-tuple-element.65), channel_id=1, source_target_pairs={{0,1},{1,2},{2,3},{3,4},{4,5},{5,6},{6,7},{7,8},{8,9},{9,10},{10,1... | collective-permute-start | bytes 196616 | tf_op jit(solution)/shard_map/ppermute | solution.py:17
  101.5 6.5 %collective-permute-start.7 = (bf16[1,64,512]{2,1,0:T(8,128)(2,1)S(1)}, bf16[1,64,512]{2,1,0:T(8,128)(2,1)S(1)}, u32[]{:S(2)}, u32[]{:S(2)}) collective-permute-start(bf16[1,64,512]{2,1,0:T(8,128)(2,1)S(1)} %get-tuple-element.66), channel_id=1, source_target_pairs={{1,0},{2,1},{3,2},{4,3},{5,4},{6,5},{7,6},{8,7},{9,8},{10,9},{11,1... | collective-permute-start | bytes 196616 | tf_op jit(solution)/shard_map/ppermute | solution.py:19
  147.2 6.3 %copy-start.1 = (bf16[1024,512]{1,0:T(8,128)(2,1)S(1)}, bf16[1024,512]{1,0:T(8,128)(2,1)}, u32[]{:S(2)}) copy-start(bf16[1024,512]{1,0:T(8,128)(2,1)} %all-gather.2.cloned.1.call-done) | copy-start | bytes 3145732
  155.6 3.3 %copy-start.5 = (bf16[2,512,512]{2,1,0:T(8,128)(2,1)S(1)}, bf16[2,512,512]{2,1,0:T(8,128)(2,1)}, u32[]{:S(2)}) copy-start(bf16[2,512,512]{2,1,0:T(8,128)(2,1)} %param.41) | copy-start | bytes 3145732
  158.9 13.0 %copy-start.6 = (bf16[64,512]{1,0:T(8,128)(2,1)}, bf16[64,512]{1,0:T(8,128)(2,1)S(1)}, u32[]{:S(2)}) copy-start(bf16[64,512]{1,0:T(8,128)(2,1)S(1)} %fusion.69) | copy-start | bytes 196612
  158.9 11.3 %copy-start.15 = (bf16[2,512,512]{2,1,0:T(8,128)(2,1)S(1)}, bf16[2,512,512]{2,1,0:T(8,128)(2,1)}, u32[]{:S(2)}) copy-start(bf16[2,512,512]{2,1,0:T(8,128)(2,1)} %param.43) | copy-start | bytes 3145732
  159.1 5.4 %collective-permute-start.8 = (bf16[1,64,512]{2,1,0:T(8,128)(2,1)S(1)}, bf16[1,64,512]{2,1,0:T(8,128)(2,1)S(1)}, u32[]{:S(2)}, u32[]{:S(2)}) collective-permute-start(bf16[1,64,512]{2,1,0:T(8,128)(2,1)S(1)} %fusion.70), channel_id=1, source_target_pairs={{0,1},{1,2},{2,3},{3,4},{4,5},{5,6},{6,7},{7,8},{8,9},{9,10},{10,1... | collective-permute-start | bytes 196616 | tf_op jit(solution)/shard_map/ppermute | solution.py:17
  162.6 6.5 %collective-permute-start.9 = (bf16[1,64,512]{2,1,0:T(8,128)(2,1)S(1)}, bf16[1,64,512]{2,1,0:T(8,128)(2,1)S(1)}, u32[]{:S(2)}, u32[]{:S(2)}) collective-permute-start(bf16[1,64,512]{2,1,0:T(8,128)(2,1)S(1)} %fusion.70), channel_id=1, source_target_pairs={{1,0},{2,1},{3,2},{4,3},{5,4},{6,5},{7,6},{8,7},{9,8},{10,9},{11,1... | collective-permute-start | bytes 196616 | tf_op jit(solution)/shard_map/ppermute | solution.py:19
  171.9 13.5 %copy-start.16 = (bf16[256,512]{1,0:T(8,128)(2,1)}, bf16[256,512]{1,0:T(8,128)(2,1)S(1)}, u32[]{:S(2)}) copy-start(bf16[256,512]{1,0:T(8,128)(2,1)S(1)} %fusion.67) | copy-start | bytes 786436
  172.3 4.3 %collective-permute-start.10 = (bf16[1,128,512]{2,1,0:T(8,128)(2,1)S(1)}, bf16[1,128,512]{2,1,0:T(8,128)(2,1)S(1)}, u32[]{:S(2)}, u32[]{:S(2)}) collective-permute-start(bf16[1,128,512]{2,1,0:T(8,128)(2,1)S(1)} %get-tuple-element.61), channel_id=1, source_target_pairs={{0,1},{1,2},{2,3},{3,4},{4,5},{5,6},{6,7},{7,8},{8,9},{9,10},{10,1... | collective-permute-start | bytes 393224 | tf_op jit(solution)/shard_map/ppermute | solution.py:17
  174.2 7.2 %collective-permute-start.11 = (bf16[1,128,512]{2,1,0:T(8,128)(2,1)S(1)}, bf16[1,128,512]{2,1,0:T(8,128)(2,1)S(1)}, u32[]{:S(2)}, u32[]{:S(2)}) collective-permute-start(bf16[1,128,512]{2,1,0:T(8,128)(2,1)S(1)} %get-tuple-element.62), channel_id=1, source_target_pairs={{1,0},{2,1},{3,2},{4,3},{5,4},{6,5},{7,6},{8,7},{9,8},{10,9},{11,1... | collective-permute-start | bytes 393224 | tf_op jit(solution)/shard_map/ppermute | solution.py:19
Sparse Core Ops, SparseCore 0:
  110.2 36.9 all-gather.1
where the time goes:
time: 198 us; the launch traced here: 197 us
  waiting for transfers between devices  60.4 us (31%)
  local copies, waits for them, and re-layouts  54.7 us (28%)
  matrix products  36.1 us (18%)
  starting transfers between devices  28.6 us (14%)
  between operations  14.9 us (8%)
    gather x12, local copies, waits for them, and re-layouts, process_local(): fetched = extended[local_ids[:, slot_index]].astype(jnp.float32)  40.9 us
    all_gather x1, waiting for transfers between devices, local(): fragment = lax.all_gather(peer_proj, 'tile', axis=0, tiled=True)  36.7 us
    ppermute x6, waiting for transfers between devices, with_halo(): lax.ppermute(head, axis, [((i + 1) % count, i) for i in range(ends)])  23.7 us
    ppermute x6, starting transfers between devices, with_halo(): lax.ppermute(tail, axis, [(i, (i + 1) % count) for i in range(ends)])  14.9 us
    ppermute x6, starting transfers between devices, with_halo(): lax.ppermute(head, axis, [((i + 1) % count, i) for i in range(ends)])  13.6 us
    dot_general x1, matrix products, finish_level(): jnp.dot(message, node_message[level_index], preferred_element_type=jnp.fl...  9.98 us
    gather x6, local copies, waits for them, and re-layouts, local(): fragment[jnp.clip(where_ids, 0, row_count - 1)].astype(jnp.float32)  8.41 us
    dot_general x3, matrix products, finish_level(): jnp.dot(hidden, node_out[level_index], preferred_element_type=jnp.float32)  6.61 us
  transfers between devices with their start and end apart: 13, of which 7 were waited for; matrix products, arithmetic and copies ran while one was open for 3% of the time, Pallas kernels for 0%

commit v1 on v0

--- a/solution.py
+++ b/solution.py
@@ -135,6 +135,15 @@
     down_bias,
     down_out,
 ):
+
+    def shape_plate(u):
+        return jnp.concatenate(
+            lax.all_to_all(
+                jnp.stack(tuple((u for _ in range(lax.axis_size("tile")))), axis=0), "tile", 0, 0
+            ),
+            axis=0,
+        )
+
     weights = (edge_self, edge_peer, edge_bias, node_self, node_message, node_bias, node_out)
     downs = (down_self, down_parent, down_bias, down_out)
     col_mid = COLS // 2
@@ -150,7 +159,7 @@
         coarse_table, lax.axis_index("tile") * coarse_count, coarse_count, 0
     )
     running = jnp.zeros(own_proj.shape, jnp.float32)
-    fragment = lax.all_gather(peer_proj, "tile", axis=0, tiled=True)
+    fragment = shape_plate(peer_proj)
     row_count = fragment.shape[0]
     for slot_index in range(6):
         where_ids = my_table[:, slot_index]

time: 198 us -> 173 us (0.87)
  waiting for transfers between devices: 60.4 us -> 46.8 us
  between operations: 14.9 us -> 1.49 us
  starting transfers between devices: 28.6 us -> 34.3 us
  local copies, waits for them, and re-layouts: 54.7 us -> 51.6 us
    all_gather x1 -> x0, waiting for transfers between devices: 36.7 us -> none  [local(): fragment = lax.all_gather(peer_proj, 'tile', axis=0, tiled=True)]
    all_to_all x0 -> x1, waiting for transfers between devices: none -> 23.1 us  [shape_plate(): lax.all_to_all(jnp.stack(tuple((u for _ in range(lax.axis_size('tile'))))...]
    all_to_all x0 -> x1, starting transfers between devices: none -> 5.06 us  [shape_plate(): lax.all_to_all(jnp.stack(tuple((u for _ in range(lax.axis_size('tile'))))...]
    gather x6, local copies, waits for them, and re-layouts: 8.41 us -> 4.21 us  [local(): fragment[jnp.clip(where_ids, 0, row_count - 1)].astype(jnp.float32)]
where the time goes in v1:
time: 173 us; the launch traced here: 172 us
  local copies, waits for them, and re-layouts  51.6 us (30%)
  waiting for transfers between devices  46.8 us (27%)
  matrix products  35.5 us (21%)
  starting transfers between devices  34.3 us (20%)
  other arithmetic  1.88 us (1%)
    gather x12, local copies, waits for them, and re-layouts, process_local(): fetched = extended[local_ids[:, slot_index]].astype(jnp.float32)  40.9 us
    ppermute x6, waiting for transfers between devices, with_halo(): lax.ppermute(head, axis, [((i + 1) % count, i) for i in range(ends)])  23.7 us
    all_to_all x1, waiting for transfers between devices, shape_plate(): lax.all_to_all(jnp.stack(tuple((u for _ in range(lax.axis_size('tile'))))...  23.1 us
    ppermute x6, starting transfers between devices, with_halo(): lax.ppermute(tail, axis, [(i, (i + 1) % count) for i in range(ends)])  15.6 us
    ppermute x6, starting transfers between devices, with_halo(): lax.ppermute(head, axis, [((i + 1) % count, i) for i in range(ends)])  13.6 us
    dot_general x1, matrix products, finish_level(): jnp.dot(message, node_message[level_index], preferred_element_type=jnp.fl...  9.98 us
    dot_general x3, matrix products, finish_level(): jnp.dot(hidden, node_out[level_index], preferred_element_type=jnp.float32)  6.61 us
    dot_general x2, matrix products, descend_local(): jnp.dot(hidden, down_out[level_index], preferred_element_type=jnp.float32)  6.04 us
  transfers between devices with their start and end apart: 13, of which 7 were waited for; matrix products, arithmetic and copies ran while one was open for 3% of the time, Pallas kernels for 0%

profile of v1, /device:TPU:5, one launch (start us, length us, event | category | flops | bytes accessed | tf_op | source)
XLA Modules:
  0.0 171.6 jit_solution(11951607838813817216)
XLA Ops:
  0.7 2.1 %convolution_convert_fusion = bf16[1024,512]{1,0:T(8,128)(2,1)S(1)} fusion(bf16[1024,512]{1,0:T(8,128)(2,1)} %param.26, bf16[3,512,512]{2,1,0:T(8,128)(2,1)} %param.33), kind=kOutput, calls=%fused_computation.97 | convolution fusion | flops 537395200 | bytes 2621440 | tf_op jit(solution)/shard_map/dot_general | solution.py:64
  2.9 3.8 %collective-permute-start = (bf16[1,256,512]{2,1,0:T(8,128)(2,1)S(1)}, bf16[1,256,512]{2,1,0:T(8,128)(2,1)S(1)}, u32[]{:S(2)}, u32[]{:S(2)}) collective-permute-start(bf16[1,256,512]{2,1,0:T(8,128)(2,1)S(1)} %get-tuple-element.57), channel_id=1, source_target_pairs={{0,1},{1,2},{2,3},{3,4},{4,5},{5,6},{6,7},{7,8},{8,9},{9,10},{10,1... | collective-permute-start | bytes 786440 | tf_op jit(solution)/shard_map/ppermute | solution.py:17
  6.8 1.9 %collective-permute-start.1 = (bf16[1,256,512]{2,1,0:T(8,128)(2,1)S(1)}, bf16[1,256,512]{2,1,0:T(8,128)(2,1)S(1)}, u32[]{:S(2)}, u32[]{:S(2)}) collective-permute-start(bf16[1,256,512]{2,1,0:T(8,128)(2,1)S(1)} %get-tuple-element.58), channel_id=1, source_target_pairs={{1,0},{2,1},{3,2},{4,3},{5,4},{6,5},{7,6},{8,7},{9,8},{10,9},{11,1... | collective-permute-start | bytes 786440 | tf_op jit(solution)/shard_map/ppermute | solution.py:19
  8.9 3.1 %fusion.175 = f32[1024,512]{1,0:T(8,128)} fusion(bf16[1024,512]{1,0:T(8,128)(2,1)S(1)} %copy-done.2, bf16[3,512,512]{2,1,0:T(8,128)(2,1)} %param.35), kind=kOutput, calls=%fused_computation.221 | convolution fusion | flops 536870912 | bytes 3670016 | tf_op jit(solution)/shard_map/dot_general | solution.py:43
  12.2 3.2 %collective-permute-done.1 = bf16[1,256,512]{2,1,0:T(8,128)(2,1)S(1)} collective-permute-done((bf16[1,256,512]{2,1,0:T(8,128)(2,1)S(1)}, bf16[1,256,512]{2,1,0:T(8,128)(2,1)S(1)}, u32[]{:S(2)}, u32[]{:S(2)}) %collective-permute-start.1) | collective-permute-done | bytes 262176 | tf_op jit(solution)/shard_map/ppermute | solution.py:19
  15.4 0.2 pad_maximum_fusion
  15.6 5.1 %gather_fusion = bf16[1024,512]{1,0:T(8,128)(2,1)} fusion(bf16[1536,512]{1,0:T(8,128)(2,1)S(1)} %bitcast.202, s32[1024]{0:T(1024)S(1)} %broadcast_clamp_fusion.5), kind=kCustom, calls=%fused_computation | custom fusion | bytes 2101248 | tf_op jit(solution)/shard_map/gather | solution.py:76
  20.6 5.1 %gather_fusion.1 = bf16[1024,512]{1,0:T(8,128)(2,1)} fusion(bf16[1536,512]{1,0:T(8,128)(2,1)S(1)} %bitcast.203, s32[1024]{0:T(1024)S(1)} %broadcast_clamp_fusion.4), kind=kCustom, calls=%fused_computation.1 | custom fusion | bytes 2101248 | tf_op jit(solution)/shard_map/gather | solution.py:76
  25.7 5.1 %gather_fusion.2 = bf16[1024,512]{1,0:T(8,128)(2,1)} fusion(bf16[1536,512]{1,0:T(8,128)(2,1)S(1)} %bitcast.204, s32[1024]{0:T(1024)S(1)} %broadcast_clamp_fusion.3), kind=kCustom, calls=%fused_computation.2 | custom fusion | bytes 2101248 | tf_op jit(solution)/shard_map/gather | solution.py:76
  30.8 5.0 %gather_fusion.3 = bf16[1024,512]{1,0:T(8,128)(2,1)} fusion(bf16[1536,512]{1,0:T(8,128)(2,1)S(1)} %bitcast.205, s32[1024]{0:T(1024)S(1)} %broadcast_clamp_fusion.2), kind=kCustom, calls=%fused_computation.3 | custom fusion | bytes 2101248 | tf_op jit(solution)/shard_map/gather | solution.py:76
  35.8 5.1 %gather_fusion.4 = bf16[1024,512]{1,0:T(8,128)(2,1)} fusion(bf16[1536,512]{1,0:T(8,128)(2,1)S(1)} %bitcast.206, s32[1024]{0:T(1024)S(1)} %broadcast_clamp_fusion.1), kind=kCustom, calls=%fused_computation.4 | custom fusion | bytes 2101248 | tf_op jit(solution)/shard_map/gather | solution.py:76
  40.9 5.1 %gather_fusion.5 = bf16[1024,512]{1,0:T(8,128)(2,1)} fusion(bf16[1536,512]{1,0:T(8,128)(2,1)S(1)} %bitcast.207, s32[1024]{0:T(1024)S(1)} %broadcast_clamp_fusion), kind=kCustom, calls=%fused_computation.5 | custom fusion | bytes 2101248 | tf_op jit(solution)/shard_map/gather | solution.py:76
  46.0 10.0 %fusion.54 = bf16[1024,512]{1,0:T(8,128)(2,1)S(1)} fusion(f32[1024,512]{1,0:T(8,128)} %fusion.175, f32[512]{0:T(512)S(1)} %bitcast.253, bf16[1024,512]{1,0:T(8,128)(2,1)} %gather_fusion.5, bf16[1024,512]{1,0:T(8,128)(2,1)} %gather_fusion.4, bf16[1024,512]{1,0:T(8,128)(2,1)} %gather_fusion.3, bf16[1024,512]{1,0:T(8,128)(2,1)} %gather_fusion.2, ...), kind=kOutput, calls=%fused_computation.82 | convolution fusion | flops 1114636288 | bytes 11538432 | tf_op jit(solution)/shard_map/dot_general | solution.py:46
  56.0 1.7 %add_convert_fusion.1 = bf16[1024,512]{1,0:T(8,128)(2,1)S(1)} fusion(bf16[1024,512]{1,0:T(8,128)(2,1)S(1)} %copy-done.3, bf16[1024,512]{1,0:T(8,128)(2,1)S(1)} %fusion.54, bf16[3,512,512]{2,1,0:T(8,128)(2,1)} %param.38), kind=kOutput, calls=%fused_computation.93 | convolution fusion | flops 538443776 | bytes 3670016 | tf_op jit(solution)/shard_map/dot_general | solution.py:50
  57.7 0.7 fusion.343
  58.5 1.9 %collective-permute-start.2 = (bf16[1,128,512]{2,1,0:T(8,128)(2,1)S(1)}, bf16[1,128,512]{2,1,0:T(8,128)(2,1)S(1)}, u32[]{:S(2)}, u32[]{:S(2)}) collective-permute-start(bf16[1,128,512]{2,1,0:T(8,128)(2,1)S(1)} %get-tuple-element.59), channel_id=1, source_target_pairs={{0,1},{1,2},{2,3},{3,4},{4,5},{5,6},{6,7},{7,8},{8,9},{9,10},{10,1... | collective-permute-start | bytes 393224 | tf_op jit(solution)/shard_map/ppermute | solution.py:17
  60.4 2.6 %collective-permute-start.3 = (bf16[1,128,512]{2,1,0:T(8,128)(2,1)S(1)}, bf16[1,128,512]{2,1,0:T(8,128)(2,1)S(1)}, u32[]{:S(2)}, u32[]{:S(2)}) collective-permute-start(bf16[1,128,512]{2,1,0:T(8,128)(2,1)S(1)} %get-tuple-element.60), channel_id=1, source_target_pairs={{1,0},{2,1},{3,2},{4,3},{5,4},{6,5},{7,6},{8,7},{9,8},{10,9},{11,1... | collective-permute-start | bytes 393224 | tf_op jit(solution)/shard_map/ppermute | solution.py:19
  63.1 4.5 %collective-permute-done.3 = bf16[1,128,512]{2,1,0:T(8,128)(2,1)S(1)} collective-permute-done((bf16[1,128,512]{2,1,0:T(8,128)(2,1)S(1)}, bf16[1,128,512]{2,1,0:T(8,128)(2,1)S(1)}, u32[]{:S(2)}, u32[]{:S(2)}) %collective-permute-start.3) | collective-permute-done | bytes 131104 | tf_op jit(solution)/shard_map/ppermute | solution.py:19
  67.7 0.1 multiply_reduce_fusion
  67.8 0.1 multiply_convert_fusion
  68.0 1.5 convolution_convert_fusion.2
  69.5 0.3 fusion.160
  69.8 1.9 %collective-permute-start.4 = (bf16[1,128,512]{2,1,0:T(8,128)(2,1)S(1)}, bf16[1,128,512]{2,1,0:T(8,128)(2,1)S(1)}, u32[]{:S(2)}, u32[]{:S(2)}) collective-permute-start(bf16[1,128,512]{2,1,0:T(8,128)(2,1)S(1)} %get-tuple-element.63), channel_id=1, source_target_pairs={{0,1},{1,2},{2,3},{3,4},{4,5},{5,6},{6,7},{7,8},{8,9},{9,10},{10,1... | collective-permute-start | bytes 393224 | tf_op jit(solution)/shard_map/ppermute | solution.py:17
  71.7 2.4 %collective-permute-start.5 = (bf16[1,128,512]{2,1,0:T(8,128)(2,1)S(1)}, bf16[1,128,512]{2,1,0:T(8,128)(2,1)S(1)}, u32[]{:S(2)}, u32[]{:S(2)}) collective-permute-start(bf16[1,128,512]{2,1,0:T(8,128)(2,1)S(1)} %get-tuple-element.64), channel_id=1, source_target_pairs={{1,0},{2,1},{3,2},{4,3},{5,4},{6,5},{7,6},{8,7},{9,8},{10,9},{11,1... | collective-permute-start | bytes 393224 | tf_op jit(solution)/shard_map/ppermute | solution.py:19
  74.1 1.3 convolution_add_fusion.3
  75.5 0.8 fusion.163
  76.3 2.6 %collective-permute-done.5 = bf16[1,128,512]{2,1,0:T(8,128)(2,1)S(1)} collective-permute-done((bf16[1,128,512]{2,1,0:T(8,128)(2,1)S(1)}, bf16[1,128,512]{2,1,0:T(8,128)(2,1)S(1)}, u32[]{:S(2)}, u32[]{:S(2)}) %collective-permute-start.5) | collective-permute-done | bytes 131104 | tf_op jit(solution)/shard_map/ppermute | solution.py:19
  79.0 1.2 gather_fusion.10
  80.1 1.9 %gather_fusion.6 = bf16[256,512]{1,0:T(8,128)(2,1)} fusion(bf16[512,512]{1,0:T(8,128)(2,1)S(1)} %bitcast.209, s32[1024]{0:T(1024)S(1)} %pad_clamp_fusion.12), kind=kCustom, calls=%fused_computation.6 | custom fusion | bytes 525312 | tf_op jit(solution)/shard_map/gather | solution.py:76
  82.0 1.9 %gather_fusion.7 = bf16[256,512]{1,0:T(8,128)(2,1)} fusion(bf16[512,512]{1,0:T(8,128)(2,1)S(1)} %bitcast.210, s32[1024]{0:T(1024)S(1)} %pad_clamp_fusion.11), kind=kCustom, calls=%fused_computation.7 | custom fusion | bytes 525312 | tf_op jit(solution)/shard_map/gather | solution.py:76
  83.8 1.9 %gather_fusion.8 = bf16[256,512]{1,0:T(8,128)(2,1)} fusion(bf16[512,512]{1,0:T(8,128)(2,1)S(1)} %bitcast.211, s32[1024]{0:T(1024)S(1)} %pad_clamp_fusion.10), kind=kCustom, calls=%fused_computation.8 | custom fusion | bytes 525312 | tf_op jit(solution)/shard_map/gather | solution.py:76
  85.7 1.9 %gather_fusion.9 = bf16[256,512]{1,0:T(8,128)(2,1)} fusion(bf16[512,512]{1,0:T(8,128)(2,1)S(1)} %bitcast.212, s32[1024]{0:T(1024)S(1)} %pad_clamp_fusion.9), kind=kCustom, calls=%fused_computation.9 | custom fusion | bytes 525312 | tf_op jit(solution)/shard_map/gather | solution.py:76
  87.6 1.9 %gather_fusion.11 = bf16[256,512]{1,0:T(8,128)(2,1)} fusion(bf16[512,512]{1,0:T(8,128)(2,1)S(1)} %bitcast.213, s32[1024]{0:T(1024)S(1)} %pad_clamp_fusion.7), kind=kCustom, calls=%fused_computation.11 | custom fusion | bytes 525312 | tf_op jit(solution)/shard_map/gather | solution.py:76
  89.4 3.3 %fusion.66 = bf16[256,512]{1,0:T(8,128)(2,1)S(1)} fusion(f32[256,512]{1,0:T(8,128)S(1)} %fusion.160, bf16[3,512,512]{2,1,0:T(8,128)(2,1)} %param.38, bf16[3,512,512]{2,1,0:T(8,128)(2,1)} %param.36, bf16[256,512]{1,0:T(8,128)(2,1)} %fusion.163, f32[256,512]{1,0:T(8,128)S(1)} %convolution_add_fusion.3, bf16[256,512]{1,0:T(8,128)(2,1)} %gather_fusion.11, ...), kind=kOutput, calls=%fused_computation.103 | convolution fusion | flops 278921216 | bytes 4196352 | tf_op jit(solution)/shard_map/dot_general | solution.py:50
  92.7 0.2 fusion.344
  93.0 1.9 %collective-permute-start.6 = (bf16[1,64,512]{2,1,0:T(8,128)(2,1)S(1)}, bf16[1,64,512]{2,1,0:T(8,128)(2,1)S(1)}, u32[]{:S(2)}, u32[]{:S(2)}) collective-permute-start(bf16[1,64,512]{2,1,0:T(8,128)(2,1)S(1)} %get-tuple-element.65), channel_id=1, source_target_pairs={{0,1},{1,2},{2,3},{3,4},{4,5},{5,6},{6,7},{7,8},{8,9},{9,10},{10,1... | collective-permute-start | bytes 196616 | tf_op jit(solution)/shard_map/ppermute | solution.py:17
  94.9 2.4 %collective-permute-start.7 = (bf16[1,64,512]{2,1,0:T(8,128)(2,1)S(1)}, bf16[1,64,512]{2,1,0:T(8,128)(2,1)S(1)}, u32[]{:S(2)}, u32[]{:S(2)}) collective-permute-start(bf16[1,64,512]{2,1,0:T(8,128)(2,1)S(1)} %get-tuple-element.66), channel_id=1, source_target_pairs={{1,0},{2,1},{3,2},{4,3},{5,4},{6,5},{7,6},{8,7},{9,8},{10,9},{11,1... | collective-permute-start | bytes 196616 | tf_op jit(solution)/shard_map/ppermute | solution.py:19
  97.3 4.1 %collective-permute-done.7 = bf16[1,64,512]{2,1,0:T(8,128)(2,1)S(1)} collective-permute-done((bf16[1,64,512]{2,1,0:T(8,128)(2,1)S(1)}, bf16[1,64,512]{2,1,0:T(8,128)(2,1)S(1)}, u32[]{:S(2)}, u32[]{:S(2)}) %collective-permute-start.7) | collective-permute-done | bytes 65568 | tf_op jit(solution)/shard_map/ppermute | solution.py:19
  101.4 0.1 multiply_reduce_fusion.1
  101.6 1.2 convolution_convert_fusion.4
  102.9 1.1 stack.2
  103.9 5.1 %all-to-all-start = ((bf16[16,64,512]{2,1,0:T(8,128)(2,1)}), bf16[16,64,512]{2,1,0:T(8,128)(2,1)S(1)}, u32[]{:S(2)}, u32[]{:S(2)}) async-start(bf16[16,64,512]{2,1,0:T(8,128)(2,1)} %stack.2), calls=%async_computation | async-start | bytes 2097152 | tf_op jit(solution)/shard_map/all_to_all | solution.py:141
  109.2 0.2 fusion.151
  109.4 23.1 %all-to-all-done = bf16[16,64,512]{2,1,0:T(8,128)(2,1)S(1)} async-done(((bf16[16,64,512]{2,1,0:T(8,128)(2,1)}), bf16[16,64,512]{2,1,0:T(8,128)(2,1)S(1)}, u32[]{:S(2)}, u32[]{:S(2)}) %all-to-all-start) | async-done | bytes 1048608 | tf_op jit(solution)/shard_map/all_to_all | solution.py:141
  132.5 0.7 gather_fusion.12
  133.2 0.7 gather_fusion.13
  133.9 0.7 gather_fusion.14
  134.6 0.7 gather_fusion.15
  135.3 0.7 gather_fusion.16
  136.0 0.7 gather_fusion.17
  136.7 1.7 fusion.297
  138.4 1.6 fusion.69
  140.1 0.2 fusion.70
  140.3 4.1 %collective-permute-start.8 = (bf16[1,64,512]{2,1,0:T(8,128)(2,1)S(1)}, bf16[1,64,512]{2,1,0:T(8,128)(2,1)S(1)}, u32[]{:S(2)}, u32[]{:S(2)}) collective-permute-start(bf16[1,64,512]{2,1,0:T(8,128)(2,1)S(1)} %fusion.70), channel_id=1, source_target_pairs={{0,1},{1,2},{2,3},{3,4},{4,5},{5,6},{6,7},{7,8},{8,9},{9,10},{10,1... | collective-permute-start | bytes 196616 | tf_op jit(solution)/shard_map/ppermute | solution.py:17
  144.3 1.9 %collective-permute-start.9 = (bf16[1,64,512]{2,1,0:T(8,128)(2,1)S(1)}, bf16[1,64,512]{2,1,0:T(8,128)(2,1)S(1)}, u32[]{:S(2)}, u32[]{:S(2)}) collective-permute-start(bf16[1,64,512]{2,1,0:T(8,128)(2,1)S(1)} %fusion.70), channel_id=1, source_target_pairs={{1,0},{2,1},{3,2},{4,3},{5,4},{6,5},{7,6},{8,7},{9,8},{10,9},{11,1... | collective-permute-start | bytes 196616 | tf_op jit(solution)/shard_map/ppermute | solution.py:19
  146.3 4.5 %collective-permute-done.9 = bf16[1,64,512]{2,1,0:T(8,128)(2,1)S(1)} collective-permute-done((bf16[1,64,512]{2,1,0:T(8,128)(2,1)S(1)}, bf16[1,64,512]{2,1,0:T(8,128)(2,1)S(1)}, u32[]{:S(2)}, u32[]{:S(2)}) %collective-permute-start.9) | collective-permute-done | bytes 65568 | tf_op jit(solution)/shard_map/ppermute | solution.py:19
  150.9 1.2 gather_fusion.18
  152.0 1.7 fusion.67
  153.7 0.3 convolution_convert_fusion.1
  154.1 1.9 %collective-permute-start.10 = (bf16[1,128,512]{2,1,0:T(8,128)(2,1)S(1)}, bf16[1,128,512]{2,1,0:T(8,128)(2,1)S(1)}, u32[]{:S(2)}, u32[]{:S(2)}) collective-permute-start(bf16[1,128,512]{2,1,0:T(8,128)(2,1)S(1)} %get-tuple-element.61), channel_id=1, source_target_pairs={{0,1},{1,2},{2,3},{3,4},{4,5},{5,6},{6,7},{7,8},{8,9},{9,10},{10,1... | collective-permute-start | bytes 393224 | tf_op jit(solution)/shard_map/ppermute | solution.py:17
  156.0 2.4 %collective-permute-start.11 = (bf16[1,128,512]{2,1,0:T(8,128)(2,1)S(1)}, bf16[1,128,512]{2,1,0:T(8,128)(2,1)S(1)}, u32[]{:S(2)}, u32[]{:S(2)}) collective-permute-start(bf16[1,128,512]{2,1,0:T(8,128)(2,1)S(1)} %get-tuple-element.62), channel_id=1, source_target_pairs={{1,0},{2,1},{3,2},{4,3},{5,4},{6,5},{7,6},{8,7},{9,8},{10,9},{11,1... | collective-permute-start | bytes 393224 | tf_op jit(solution)/shard_map/ppermute | solution.py:19
  158.4 4.8 %collective-permute-done.11 = bf16[1,128,512]{2,1,0:T(8,128)(2,1)S(1)} collective-permute-done((bf16[1,128,512]{2,1,0:T(8,128)(2,1)S(1)}, bf16[1,128,512]{2,1,0:T(8,128)(2,1)S(1)}, u32[]{:S(2)}, u32[]{:S(2)}) %collective-permute-start.11) | collective-permute-done | bytes 131104 | tf_op jit(solution)/shard_map/ppermute | solution.py:19
  163.2 4.0 %gather_fusion.19 = bf16[1024,512]{1,0:T(8,128)(2,1)S(1)} fusion(bf16[512,512]{1,0:T(8,128)(2,1)S(1)} %bitcast.214, s32[1024]{0:T(1024)S(1)} %get-tuple-element.51), kind=kCustom, calls=%fused_computation.19 | custom fusion | bytes 2101248 | tf_op jit(solution)/shard_map/gather | solution.py:105
  167.2 4.4 %add_convert_fusion = bf16[1024,512]{1,0:T(8,128)(2,1)} fusion(bf16[1024,512]{1,0:T(8,128)(2,1)} %copy-done.18, bf16[1024,512]{1,0:T(8,128)(2,1)S(1)} %gather_fusion.19, f32[512]{0:T(512)S(1)} %bitcast.251, bf16[2,512,512]{2,1,0:T(8,128)(2,1)S(1)} %copy-done.16, bf16[2,512,512]{2,1,0:T(8,128)(2,1)} %param.40), kind=kOutput, calls=%fused_computation.91 | convolution fusion | flops 1081606144 | bytes 5244928 | tf_op jit(solution)/shard_map/dot_general | solution.py:112
  (87 shorter events, 0.9 us)
Async XLA Ops:
  0.6 108.4 %copy-start = (s32[1024,6]{0,1:T(8,128)S(1)}, s32[1024,6]{0,1:T(8,128)}, u32[]{:S(2)}) copy-start(s32[1024,6]{0,1:T(8,128)} %param.29) | copy-start | bytes 73732
  0.6 8.2 %copy-start.2 = (bf16[1024,512]{1,0:T(8,128)(2,1)S(1)}, bf16[1024,512]{1,0:T(8,128)(2,1)}, u32[]{:S(2)}) copy-start(bf16[1024,512]{1,0:T(8,128)(2,1)} %param.26) | copy-start | bytes 3145732
  0.7 8.1 %copy-start.8 = (s32[1024,6]{0,1:T(8,128)S(1)}, s32[1024,6]{0,1:T(8,128)}, u32[]{:S(2)}) copy-start(s32[1024,6]{0,1:T(8,128)} %param.27) | copy-start | bytes 73732
  0.7 8.2 %copy-start.10 = (f32[3,512]{1,0:T(4,128)S(1)}, f32[3,512]{1,0:T(4,128)}, u32[]{:S(2)}) copy-start(f32[3,512]{1,0:T(4,128)} %param.37) | copy-start | bytes 18436
  2.9 9.1 %copy-start.13 = (f32[2,512]{1,0:T(2,128)S(1)}, f32[2,512]{1,0:T(2,128)}, u32[]{:S(2)}) copy-start(f32[2,512]{1,0:T(2,128)} %param.39) | copy-start | bytes 12292
  2.9 9.1 %copy-start.12 = (s32[1024]{0:T(1024)S(1)}, s32[1024]{0:T(1024)}, u32[]{:S(2)}) copy-start(s32[1024]{0:T(1024)} %param.30) | copy-start | bytes 12292
  2.9 9.1 %copy-start.9 = (s32[256,6]{0,1:T(8,128)S(1)}, s32[256,6]{0,1:T(8,128)}, u32[]{:S(2)}) copy-start(s32[256,6]{0,1:T(8,128)} %param.28) | copy-start | bytes 18436
  2.9 9.2 %copy-start.15 = (s32[256]{0:T(256)S(1)}, s32[256]{0:T(256)}, u32[]{:S(2)}) copy-start(s32[256]{0:T(256)} %param.31) | copy-start | bytes 3076
  2.9 9.2 %copy-start.11 = (f32[3,512]{1,0:T(4,128)S(1)}, f32[3,512]{1,0:T(4,128)}, u32[]{:S(2)}) copy-start(f32[3,512]{1,0:T(4,128)} %param.34) | copy-start | bytes 18436
  2.9 9.2 %collective-permute-start = (bf16[1,256,512]{2,1,0:T(8,128)(2,1)S(1)}, bf16[1,256,512]{2,1,0:T(8,128)(2,1)S(1)}, u32[]{:S(2)}, u32[]{:S(2)}) collective-permute-start(bf16[1,256,512]{2,1,0:T(8,128)(2,1)S(1)} %get-tuple-element.57), channel_id=1, source_target_pairs={{0,1},{1,2},{2,3},{3,4},{4,5},{5,6},{6,7},{7,8},{8,9},{9,10},{10,1... | collective-permute-start | bytes 786440 | tf_op jit(solution)/shard_map/ppermute | solution.py:17
  6.8 8.6 %collective-permute-start.1 = (bf16[1,256,512]{2,1,0:T(8,128)(2,1)S(1)}, bf16[1,256,512]{2,1,0:T(8,128)(2,1)S(1)}, u32[]{:S(2)}, u32[]{:S(2)}) collective-permute-start(bf16[1,256,512]{2,1,0:T(8,128)(2,1)S(1)} %get-tuple-element.58), channel_id=1, source_target_pairs={{1,0},{2,1},{3,2},{4,3},{5,4},{6,5},{7,6},{8,7},{9,8},{10,9},{11,1... | collective-permute-start | bytes 786440 | tf_op jit(solution)/shard_map/ppermute | solution.py:19
  40.9 5.1 %copy-start.3 = (bf16[1024,512]{1,0:T(8,128)(2,1)S(1)}, bf16[1024,512]{1,0:T(8,128)(2,1)}, u32[]{:S(2)}) copy-start(bf16[1024,512]{1,0:T(8,128)(2,1)} %param.26) | copy-start | bytes 3145732
  57.7 5.4 %copy-start.18 = (bf16[1024,512]{1,0:T(8,128)(2,1)}, bf16[1024,512]{1,0:T(8,128)(2,1)S(1)}, u32[]{:S(2)}) copy-start(bf16[1024,512]{1,0:T(8,128)(2,1)S(1)} %add_convert_fusion.1) | copy-start | bytes 3145732
  58.5 4.6 %collective-permute-start.2 = (bf16[1,128,512]{2,1,0:T(8,128)(2,1)S(1)}, bf16[1,128,512]{2,1,0:T(8,128)(2,1)S(1)}, u32[]{:S(2)}, u32[]{:S(2)}) collective-permute-start(bf16[1,128,512]{2,1,0:T(8,128)(2,1)S(1)} %get-tuple-element.59), channel_id=1, source_target_pairs={{0,1},{1,2},{2,3},{3,4},{4,5},{5,6},{6,7},{7,8},{8,9},{9,10},{10,1... | collective-permute-start | bytes 393224 | tf_op jit(solution)/shard_map/ppermute | solution.py:17
  60.4 7.2 %collective-permute-start.3 = (bf16[1,128,512]{2,1,0:T(8,128)(2,1)S(1)}, bf16[1,128,512]{2,1,0:T(8,128)(2,1)S(1)}, u32[]{:S(2)}, u32[]{:S(2)}) collective-permute-start(bf16[1,128,512]{2,1,0:T(8,128)(2,1)S(1)} %get-tuple-element.60), channel_id=1, source_target_pairs={{1,0},{2,1},{3,2},{4,3},{5,4},{6,5},{7,6},{8,7},{9,8},{10,9},{11,1... | collective-permute-start | bytes 393224 | tf_op jit(solution)/shard_map/ppermute | solution.py:19
  67.6 1.8 %copy-start.1 = (bf16[3,512,512]{2,1,0:T(8,128)(2,1)S(1)}, bf16[3,512,512]{2,1,0:T(8,128)(2,1)}, u32[]{:S(2)}) copy-start(bf16[3,512,512]{2,1,0:T(8,128)(2,1)} %param.35) | copy-start | bytes 4718596
  69.8 6.5 %collective-permute-start.4 = (bf16[1,128,512]{2,1,0:T(8,128)(2,1)S(1)}, bf16[1,128,512]{2,1,0:T(8,128)(2,1)S(1)}, u32[]{:S(2)}, u32[]{:S(2)}) collective-permute-start(bf16[1,128,512]{2,1,0:T(8,128)(2,1)S(1)} %get-tuple-element.63), channel_id=1, source_target_pairs={{0,1},{1,2},{2,3},{3,4},{4,5},{5,6},{6,7},{7,8},{8,9},{9,10},{10,1... | collective-permute-start | bytes 393224 | tf_op jit(solution)/shard_map/ppermute | solution.py:17
  71.7 7.2 %collective-permute-start.5 = (bf16[1,128,512]{2,1,0:T(8,128)(2,1)S(1)}, bf16[1,128,512]{2,1,0:T(8,128)(2,1)S(1)}, u32[]{:S(2)}, u32[]{:S(2)}) collective-permute-start(bf16[1,128,512]{2,1,0:T(8,128)(2,1)S(1)} %get-tuple-element.64), channel_id=1, source_target_pairs={{1,0},{2,1},{3,2},{4,3},{5,4},{6,5},{7,6},{8,7},{9,8},{10,9},{11,1... | collective-permute-start | bytes 393224 | tf_op jit(solution)/shard_map/ppermute | solution.py:19
  92.7 8.7 %copy-start.5 = (bf16[256,512]{1,0:T(8,128)(2,1)}, bf16[256,512]{1,0:T(8,128)(2,1)S(1)}, u32[]{:S(2)}) copy-start(bf16[256,512]{1,0:T(8,128)(2,1)S(1)} %fusion.66) | copy-start | bytes 786436
  93.0 4.3 %collective-permute-start.6 = (bf16[1,64,512]{2,1,0:T(8,128)(2,1)S(1)}, bf16[1,64,512]{2,1,0:T(8,128)(2,1)S(1)}, u32[]{:S(2)}, u32[]{:S(2)}) collective-permute-start(bf16[1,64,512]{2,1,0:T(8,128)(2,1)S(1)} %get-tuple-element.65), channel_id=1, source_target_pairs={{0,1},{1,2},{2,3},{3,4},{4,5},{5,6},{6,7},{7,8},{8,9},{9,10},{10,1... | collective-permute-start | bytes 196616 | tf_op jit(solution)/shard_map/ppermute | solution.py:17
  94.9 6.5 %collective-permute-start.7 = (bf16[1,64,512]{2,1,0:T(8,128)(2,1)S(1)}, bf16[1,64,512]{2,1,0:T(8,128)(2,1)S(1)}, u32[]{:S(2)}, u32[]{:S(2)}) collective-permute-start(bf16[1,64,512]{2,1,0:T(8,128)(2,1)S(1)} %get-tuple-element.66), channel_id=1, source_target_pairs={{1,0},{2,1},{3,2},{4,3},{5,4},{6,5},{7,6},{8,7},{9,8},{10,9},{11,1... | collective-permute-start | bytes 196616 | tf_op jit(solution)/shard_map/ppermute | solution.py:19
  101.5 7.7 %copy-start.14 = (f32[2,512]{1,0:T(2,128)S(1)}, f32[2,512]{1,0:T(2,128)}, u32[]{:S(2)}) copy-start(f32[2,512]{1,0:T(2,128)} %param.42) | copy-start | bytes 12292
  103.9 28.6 %all-to-all-start = ((bf16[16,64,512]{2,1,0:T(8,128)(2,1)}), bf16[16,64,512]{2,1,0:T(8,128)(2,1)S(1)}, u32[]{:S(2)}, u32[]{:S(2)}) async-start(bf16[16,64,512]{2,1,0:T(8,128)(2,1)} %stack.2), calls=%async_computation | async-start | bytes 2097152 | tf_op jit(solution)/shard_map/all_to_all | solution.py:141
  136.7 3.3 %copy-start.4 = (bf16[2,512,512]{2,1,0:T(8,128)(2,1)S(1)}, bf16[2,512,512]{2,1,0:T(8,128)(2,1)}, u32[]{:S(2)}) copy-start(bf16[2,512,512]{2,1,0:T(8,128)(2,1)} %param.41) | copy-start | bytes 3145732
  140.0 13.7 %copy-start.7 = (bf16[64,512]{1,0:T(8,128)(2,1)}, bf16[64,512]{1,0:T(8,128)(2,1)S(1)}, u32[]{:S(2)}) copy-start(bf16[64,512]{1,0:T(8,128)(2,1)S(1)} %fusion.69) | copy-start | bytes 196612
  140.0 12.0 %copy-start.6 = (bf16[256,512]{1,0:T(8,128)(2,1)S(1)}, bf16[256,512]{1,0:T(8,128)(2,1)}, u32[]{:S(2)}) copy-start(bf16[256,512]{1,0:T(8,128)(2,1)} %copy-done.5) | copy-start | bytes 786436
  140.1 12.0 %copy-start.16 = (bf16[2,512,512]{2,1,0:T(8,128)(2,1)S(1)}, bf16[2,512,512]{2,1,0:T(8,128)(2,1)}, u32[]{:S(2)}) copy-start(bf16[2,512,512]{2,1,0:T(8,128)(2,1)} %param.43) | copy-start | bytes 3145732
  140.3 6.0 %collective-permute-start.8 = (bf16[1,64,512]{2,1,0:T(8,128)(2,1)S(1)}, bf16[1,64,512]{2,1,0:T(8,128)(2,1)S(1)}, u32[]{:S(2)}, u32[]{:S(2)}) collective-permute-start(bf16[1,64,512]{2,1,0:T(8,128)(2,1)S(1)} %fusion.70), channel_id=1, source_target_pairs={{0,1},{1,2},{2,3},{3,4},{4,5},{5,6},{6,7},{7,8},{8,9},{9,10},{10,1... | collective-permute-start | bytes 196616 | tf_op jit(solution)/shard_map/ppermute | solution.py:17
  144.3 6.5 %collective-permute-start.9 = (bf16[1,64,512]{2,1,0:T(8,128)(2,1)S(1)}, bf16[1,64,512]{2,1,0:T(8,128)(2,1)S(1)}, u32[]{:S(2)}, u32[]{:S(2)}) collective-permute-start(bf16[1,64,512]{2,1,0:T(8,128)(2,1)S(1)} %fusion.70), channel_id=1, source_target_pairs={{1,0},{2,1},{3,2},{4,3},{5,4},{6,5},{7,6},{8,7},{9,8},{10,9},{11,1... | collective-permute-start | bytes 196616 | tf_op jit(solution)/shard_map/ppermute | solution.py:19
  153.7 13.5 %copy-start.17 = (bf16[256,512]{1,0:T(8,128)(2,1)}, bf16[256,512]{1,0:T(8,128)(2,1)S(1)}, u32[]{:S(2)}) copy-start(bf16[256,512]{1,0:T(8,128)(2,1)S(1)} %fusion.67) | copy-start | bytes 786436
  154.1 4.3 %collective-permute-start.10 = (bf16[1,128,512]{2,1,0:T(8,128)(2,1)S(1)}, bf16[1,128,512]{2,1,0:T(8,128)(2,1)S(1)}, u32[]{:S(2)}, u32[]{:S(2)}) collective-permute-start(bf16[1,128,512]{2,1,0:T(8,128)(2,1)S(1)} %get-tuple-element.61), channel_id=1, source_target_pairs={{0,1},{1,2},{2,3},{3,4},{4,5},{5,6},{6,7},{7,8},{8,9},{9,10},{10,1... | collective-permute-start | bytes 393224 | tf_op jit(solution)/shard_map/ppermute | solution.py:17
  156.0 7.2 %collective-permute-start.11 = (bf16[1,128,512]{2,1,0:T(8,128)(2,1)S(1)}, bf16[1,128,512]{2,1,0:T(8,128)(2,1)S(1)}, u32[]{:S(2)}, u32[]{:S(2)}) collective-permute-start(bf16[1,128,512]{2,1,0:T(8,128)(2,1)S(1)} %get-tuple-element.62), channel_id=1, source_target_pairs={{1,0},{2,1},{3,2},{4,3},{5,4},{6,5},{7,6},{8,7},{9,8},{10,9},{11,1... | collective-permute-start | bytes 393224 | tf_op jit(solution)/shard_map/ppermute | solution.py:19
